TPU v7x, 32 devices: a whole 2x2x4 slice. The times are simulated.
32 devices in a mesh: shot: 2 (over x), strip: 16 (over z, y, core).
Axes of the slice: x: 2, y: 2, z: 4, core: 2. Of those that a mesh axis runs over, the one named last changes fastest.
Arguments:
- waves: float32 [2, 2, 8, 512, 512], P(None, None, 'shot', 'strip'), parts along dimension 2, may hold values from -6 to 6
- levels: int32 [512, 512], P('strip'), may hold values from 0 to 4
- coeffs: float32 [2, 4, 5, 17], replicated, may hold values from -0.7 to 0.7
- angles: float32 [4, 5], replicated, may hold values from -3.140625 to 3.140625
- order: int32 [8], P('shot'), parts along dimension 0, may hold values from 0 to 3, each once
Outputs:
- waves_out: float32 [2, 2, 8, 512, 512], P(None, None, 'shot', 'strip'), parts along dimension 2
- image: float32 [4, 512, 512], P('shot', 'strip'), parts along dimension 0
There are 2 independent parts, one for each index of `shot`. A program takes and returns all parts, laid end to end along the dimension named above; an argument that names none is the same for every part. Nothing has to cross between parts.
Inputs may be any that keep to these rules, and one draw needn't show every extreme that they name: order names every table row once.
All inputs are finite; a program needn't handle non-finite values.
Results may differ from a plain program's by a relative error of at most 0.00013.
Values sent between devices are 32-bit elements; how exact they have to be, the bound alone decides.
A program may use at most 64 MiB of HBM per device.

v0:
```python
import functools

import jax
import jax.numpy as jnp
from jax import lax
from jax.experimental import pallas as pl
from jax.experimental.pallas import tpu as pltpu
from jax.sharding import PartitionSpec as P

STEPS = 2
LANES = 128
SUBS = 8
PAIR = 2
MESH = pl.DeviceIdType.MESH


def tile_rows(index, count=1):
    return pl.ds(pl.multiple_of(index * SUBS, SUBS), count * SUBS)


def kernel(
    sizes, waves_ref, levels_ref, coeffs_ref, angles_ref, order_ref, out_ref, image_ref,
    level_buf, coef_buf, turn_buf, field_buf, mid_buf, image_buf, send_sem, recv_sem,
):
    freqs, rows, blocks, per_tile, groups, levels, taps, strips = sizes
    half = taps // 2
    span = rows + 2 * half
    me = lax.axis_index("strip")
    has_low, has_high = me > 0, me < strips - 1

    def neighbour(step):
        return {"strip": me + step}

    barrier = pltpu.get_barrier_semaphore()
    for there, step in ((has_low, -1), (has_high, 1)):

        @pl.when(there)
        def _():
            pl.semaphore_signal(barrier, inc=1, device_id=neighbour(step), device_id_type=MESH)

    lane = lax.broadcasted_iota(jnp.int32, (SUBS, LANES), 1)
    sub = lax.broadcasted_iota(jnp.int32, (SUBS, LANES), 0)
    block_of = lax.rem(sub, blocks)

    for top in range(0, rows, SUBS):
        for block in range(blocks):
            cells = levels_ref[top : top + SUBS, block * LANES : (block + 1) * LANES]
            for member in range(per_tile):
                level_buf[pl.ds(top * SUBS + member * blocks + block, SUBS, stride=SUBS), :] = cells

    def by_member(values):
        tile = jnp.full((SUBS, LANES), values[0], jnp.float32)
        for member in range(1, per_tile):
            tile = jnp.where(sub >= member * blocks, values[member], tile)
        return tile

    slots = [order_ref[f] for f in range(freqs)]
    coef_tabs, cos_tabs, sin_tabs = [], [], []
    for group in range(groups):
        members = slots[group * per_tile : (group + 1) * per_tile]
        tabs = [jnp.zeros((SUBS, LANES), jnp.float32) for _ in range(2)]
        turn = jnp.zeros((SUBS, LANES), jnp.float32)
        for level in range(levels):
            for tap in range(taps):
                hit = lane == tap * levels + level
                for part in range(2):
                    entry = by_member([coeffs_ref[part, row, level, tap] for row in members])
                    tabs[part] = jnp.where(hit, entry, tabs[part])
            turn = jnp.where(lane == level, by_member([angles_ref[row, level] for row in members]), turn)
        coef_tabs.append(tabs)
        cos_tabs.append(jnp.cos(turn))
        sin_tabs.append(jnp.sin(turn))

    def pick(table, index):
        return jnp.take_along_axis(table, index, axis=1)

    def coef_at(group, y, tap, part):
        return tile_rows(((group * rows + y) * taps + tap) * 2 + part)

    def turn_at(group, y, which):
        return tile_rows((group * rows + y) * 2 + which)

    @pl.loop(0, rows)
    def _(y):
        level_tile = level_buf[tile_rows(y), :]
        for group in range(groups):
            turn_buf[turn_at(group, y, 0), :] = pick(cos_tabs[group], level_tile)
            turn_buf[turn_at(group, y, 1), :] = pick(sin_tabs[group], level_tile)
        for tap in range(taps):
            index = level_tile + tap * levels
            for group in range(groups):
                for part in range(2):
                    coef_buf[coef_at(group, y, tap, part), :] = pick(coef_tabs[group][part], index)

    def field_at(group, comp, y):
        return tile_rows((group * 4 + comp) * rows + y)

    def mid_at(step, group, y, comp):
        return tile_rows(((step * groups + group) * span + y) * 4 + comp)

    for group in range(groups):
        for comp in range(4):
            for member in range(per_tile):
                for top in range(0, rows, SUBS):
                    for block in range(blocks):
                        cells = waves_ref[
                            comp // 2, comp % 2, group * per_tile + member, top : top + SUBS,
                            block * LANES : (block + 1) * LANES,
                        ]
                        start = ((group * 4 + comp) * rows + top) * SUBS + member * blocks + block
                        field_buf[pl.ds(start, SUBS, stride=SUBS), :] = cells

    for there, first in ((has_low, 0), (has_high, rows + half)):

        @pl.when(jnp.logical_not(there))
        def _():
            for step in range(STEPS):
                for group in range(groups):

                    @pl.loop(0, half * 4)
                    def _(i):
                        mid_buf[tile_rows(((step * groups + group) * span + first) * 4 + i), :] = jnp.zeros(
                            (SUBS, LANES), jnp.float32
                        )

    pl.semaphore_wait(barrier, has_low.astype(jnp.int32) + has_high.astype(jnp.int32))

    def halo_copy(step, group, side):
        source, target = ((half, rows + half), (rows, 0))[side]
        base = (step * groups + group) * span
        return pltpu.make_async_remote_copy(
            src_ref=mid_buf.at[tile_rows((base + source) * 4, half * 4)],
            dst_ref=mid_buf.at[tile_rows((base + target) * 4, half * 4)],
            send_sem=send_sem.at[step, group, side],
            recv_sem=recv_sem.at[step, group, side],
            device_id=neighbour((-1, 1)[side]),
            device_id_type=MESH,
        )

    def inline_row(step, group, y):
        cosine = turn_buf[turn_at(group, y, 0), :]
        sine = turn_buf[turn_at(group, y, 1), :]
        sr, si, rr, ri = [field_buf[field_at(group, comp, y), :] for comp in range(4)]
        cells = (sr * cosine - si * sine, sr * sine + si * cosine, rr * cosine + ri * sine, ri * cosine - rr * sine)
        before = [jnp.where(block_of == 0, 0.0, pltpu.roll(v, 1, 0)) for v in cells]
        after = [jnp.where(block_of == blocks - 1, 0.0, pltpu.roll(v, SUBS - 1, 0)) for v in cells]
        acc = [None] * 4
        for tap in range(taps):
            shift = tap - half
            if shift < 0:
                moved = [
                    pltpu.roll(jnp.where(lane < LANES + shift, v, w), -shift, 1) for v, w in zip(cells, before)
                ]
            elif shift > 0:
                moved = [
                    pltpu.roll(jnp.where(lane >= shift, v, w), LANES - shift, 1) for v, w in zip(cells, after)
                ]
            else:
                moved = cells
            add_tap(acc, group, y, tap, moved)
        for comp in range(4):
            mid_buf[mid_at(step, group, y + half, comp), :] = acc[comp]

    def add_tap(acc, group, y, tap, moved):
        cr = coef_buf[coef_at(group, y, tap, 0), :]
        ci = coef_buf[coef_at(group, y, tap, 1), :]
        sr, si, rr, ri = moved
        if acc[0] is None:
            acc[:] = [cr * sr - ci * si, cr * si + ci * sr, cr * rr + ci * ri, cr * ri - ci * rr]
        else:
            acc[0] = acc[0] + cr * sr - ci * si
            acc[1] = acc[1] + cr * si + ci * sr
            acc[2] = acc[2] + cr * rr + ci * ri
            acc[3] = acc[3] + cr * ri - ci * rr

    def inline_pass(step, group):
        @pl.loop(0, half)
        def _(y):
            inline_row(step, group, y)

        @pl.loop(rows - half, rows)
        def _(y):
            inline_row(step, group, y)

        for side, there in enumerate((has_low, has_high)):

            @pl.when(there)
            def _():
                halo_copy(step, group, side).start()

        @pl.loop(half, rows - half)
        def _(y):
            inline_row(step, group, y)

    def cross_pass(step, group):
        for side, there in ((1, has_low), (0, has_high)):

            @pl.when(there)
            def _():
                halo_copy(step, group, side).wait_recv()

        @pl.loop(0, rows // PAIR)
        def _(trip):
            y = trip * PAIR
            accs = [[None] * 4 for _ in range(PAIR)]
            for line in range(taps + PAIR - 1):
                moved = [mid_buf[mid_at(step, group, y + line, comp), :] for comp in range(4)]
                for place in range(PAIR):
                    if 0 <= line - place < taps:
                        add_tap(accs[place], group, y + place, line - place, moved)
            for place, acc in enumerate(accs):
                for comp in range(4):
                    field_buf[field_at(group, comp, y + place), :] = acc[comp]
                term = acc[0] * acc[2] + acc[1] * acc[3]
                at = tile_rows(step * rows + y + place)
                if group == 0:
                    image_buf[at, :] = term
                else:
                    image_buf[at, :] = image_buf[at, :] + term

    for step in range(STEPS):
        for group in range(groups):
            inline_pass(step, group)
        for group in range(groups):
            cross_pass(step, group)

    for group in range(groups):
        for comp in range(4):
            for member in range(per_tile):
                for top in range(0, rows, SUBS):
                    for block in range(blocks):
                        start = ((group * 4 + comp) * rows + top) * SUBS + member * blocks + block
                        out_ref[
                            comp // 2, comp % 2, group * per_tile + member, top : top + SUBS,
                            block * LANES : (block + 1) * LANES,
                        ] = field_buf[pl.ds(start, SUBS, stride=SUBS), :]
    for step in range(STEPS):
        for top in range(0, rows, SUBS):
            for block in range(blocks):
                total = None
                for member in range(per_tile):
                    start = (step * rows + top) * SUBS + member * blocks + block
                    term = image_buf[pl.ds(start, SUBS, stride=SUBS), :]
                    total = term if total is None else total + term
                image_ref[step, top : top + SUBS, block * LANES : (block + 1) * LANES] = total

    for step in range(STEPS):
        for group in range(groups):
            for side, there in enumerate((has_low, has_high)):

                @pl.when(there)
                def _():
                    halo_copy(step, group, side).wait_send()


def on_device(strips, waves, levels, coeffs, angles, order):
    freqs, rows, cells = waves.shape[2:]
    level_count, taps = coeffs.shape[2:]
    blocks = cells // LANES
    per_tile = SUBS // blocks
    groups = freqs // per_tile
    assert blocks * per_tile == SUBS and groups * per_tile == freqs
    assert rows % SUBS == 0 and rows >= taps - 1 and level_count * taps <= LANES
    half = taps // 2
    sizes = (freqs, rows, blocks, per_tile, groups, level_count, taps, strips)
    tiles = lambda count: pltpu.VMEM((count * SUBS, LANES), jnp.float32)
    vmem, smem = pl.BlockSpec(memory_space=pltpu.VMEM), pl.BlockSpec(memory_space=pltpu.SMEM)
    return pl.pallas_call(
        functools.partial(kernel, sizes),
        out_shape=(
            jax.ShapeDtypeStruct(waves.shape, jnp.float32),
            jax.ShapeDtypeStruct((STEPS, rows, cells), jnp.float32),
        ),
        in_specs=[vmem, vmem, smem, smem, smem],
        out_specs=(vmem, vmem),
        scratch_shapes=[
            pltpu.VMEM((rows * SUBS, LANES), jnp.int32),
            tiles(groups * rows * taps * 2),
            tiles(groups * rows * 2),
            tiles(groups * 4 * rows),
            tiles(STEPS * groups * (rows + 2 * half) * 4),
            tiles(STEPS * rows),
            pltpu.SemaphoreType.DMA((STEPS, groups, 2)),
            pltpu.SemaphoreType.DMA((STEPS, groups, 2)),
        ],
        compiler_params=pltpu.CompilerParams(
            collective_id=0, has_side_effects=True, vmem_limit_bytes=48 * 1024 * 1024
        ),
    )(waves, levels, coeffs, angles, order)


def solution(mesh):
    in_specs = (P(None, None, "shot", "strip", None), P("strip", None), P(), P(), P("shot"))
    out_specs = (P(None, None, "shot", "strip", None), P("shot", "strip", None))
    return jax.shard_map(
        functools.partial(on_device, mesh.shape["strip"]),
        mesh=mesh,
        in_specs=in_specs,
        out_specs=out_specs,
        check_vma=False,
    )
```

profile of v0, /device:TPU:9, one launch (start us, length us, event | category | flops | bytes accessed | tf_op | source)
XLA Modules:
  0.0 40.1 jit_solution(18440714627573527494)
XLA Ops:
  0.6 0.0 copy-start.3
  0.6 0.0 copy-start.2
  0.7 0.7 %copy.7.coeffs_ref = f32[2,4,5,17]{3,2,1,0:T(8,128)S(1)} copy(f32[2,4,5,17]{3,1,2,0:T(4,128)} %param.7) | data formatting | bytes 5440 | tf_op args[2]
  1.4 0.0 copy-done.3
  1.4 0.0 copy-done.2
  1.4 0.0 copy-start
  1.4 1.2 %copy-done = f32[2,2,4,32,512]{4,3,2,1,0:T(8,128)S(1)} copy-done((f32[2,2,4,32,512]{4,3,2,1,0:T(8,128)S(1)}, f32[2,2,4,32,512]{4,3,2,1,0:T(8,128)}, u32[]{:S(2)}) %copy-start) | copy-done | bytes 1048600
  2.6 0.0 copy-start.1
  2.6 0.8 %copy-done.1 = s32[32,512]{1,0:T(8,128)S(1)} copy-done((s32[32,512]{1,0:T(8,128)S(1)}, s32[32,512]{1,0:T(8,128)}, u32[]{:S(2)}) %copy-start.1) | copy-done | bytes 65560
  3.5 35.0 %shard_map.68 = (f32[2,2,4,32,512]{4,3,2,1,0:T(8,128)S(1)}, f32[2,32,512]{2,1,0:T(8,128)S(1)}) custom-call(f32[2,2,4,32,512]{4,3,2,1,0:T(8,128)S(1)} %copy-done, s32[32,512]{1,0:T(8,128)S(1)} %copy-done.1, f32[2,4,5,17]{3,2,1,0:T(8,128)S(1)} %copy.7.coeffs_ref, f32[4,5]{1,0:T(4,128)S(1)} %copy-done.2, s32[4]{0:T(128)S(1)} %copy-done.3), custom_call_target="tpu_custom_call" | custom-call | tf_op jit(solution)/shard_map/pallas_call | solution.py:268
  38.5 1.0 %copy.10 = f32[2,2,4,32,512]{4,3,2,1,0:T(8,128)} copy(f32[2,2,4,32,512]{4,3,2,1,0:T(8,128)S(1)} %get-tuple-element.4) | data formatting | bytes 2097152
  39.4 0.7 %copy.11 = f32[2,32,512]{2,1,0:T(8,128)} copy(f32[2,32,512]{2,1,0:T(8,128)S(1)} %get-tuple-element.5) | data formatting | bytes 262144
Async XLA Ops:
  0.6 0.8 %copy-start.3 = (s32[4]{0:T(128)S(1)}, s32[4]{0:T(128)}, u32[]{:S(2)}) copy-start(s32[4]{0:T(128)} %order_ref.1) | copy-start | bytes 52
  0.6 0.8 %copy-start.2 = (f32[4,5]{1,0:T(4,128)S(1)}, f32[4,5]{1,0:T(4,128)}, u32[]{:S(2)}) copy-start(f32[4,5]{1,0:T(4,128)} %angles_ref.1) | copy-start | bytes 244
  1.4 1.2 %copy-start = (f32[2,2,4,32,512]{4,3,2,1,0:T(8,128)S(1)}, f32[2,2,4,32,512]{4,3,2,1,0:T(8,128)}, u32[]{:S(2)}) copy-start(f32[2,2,4,32,512]{4,3,2,1,0:T(8,128)} %waves_ref.1) | copy-start | bytes 3145732
  2.6 0.8 %copy-start.1 = (s32[32,512]{1,0:T(8,128)S(1)}, s32[32,512]{1,0:T(8,128)}, u32[]{:S(2)}) copy-start(s32[32,512]{1,0:T(8,128)} %levels_ref.1) | copy-start | bytes 196612
where the time goes:
time: 40.3 us; the launch traced here: 40.1 us
  Pallas kernels  35 us (87%)
  local copies, waits for them, and re-layouts  4.44 us (11%)
  between operations  0.67 us (2%)
    pallas_call x1, Pallas kernels, on_device(): pl.pallas_call(functools.partial(kernel, sizes), out_shape=(jax.ShapeDtyp...  35 us
    unnamed x11, local copies, waits for them, and re-layouts  4.44 us

commit v1 on v0

--- a/solution.py
+++ b/solution.py
@@ -10,6 +10,7 @@
 STEPS = 2
 LANES = 128
 SUBS = 8
+ROWS = 2
 PAIR = 2
 MESH = pl.DeviceIdType.MESH
 
@@ -20,7 +21,7 @@
 
 def kernel(
     sizes, waves_ref, levels_ref, coeffs_ref, angles_ref, order_ref, out_ref, image_ref,
-    level_buf, coef_buf, turn_buf, field_buf, mid_buf, image_buf, send_sem, recv_sem,
+    level_buf, table_buf, coef_buf, turn_buf, field_buf, mid_buf, image_buf, send_sem, recv_sem,
 ):
     freqs, rows, blocks, per_tile, groups, levels, taps, strips = sizes
     half = taps // 2
@@ -48,6 +49,9 @@
             for member in range(per_tile):
                 level_buf[pl.ds(top * SUBS + member * blocks + block, SUBS, stride=SUBS), :] = cells
 
+    def table_at(group, tap, part, level):
+        return tile_rows(((group * taps + tap) * 2 + part) * levels + level)
+
     def by_member(values):
         tile = jnp.full((SUBS, LANES), values[0], jnp.float32)
         for member in range(1, per_tile):
@@ -55,24 +59,19 @@
         return tile
 
     slots = [order_ref[f] for f in range(freqs)]
-    coef_tabs, cos_tabs, sin_tabs = [], [], []
+    turn_tabs = []
     for group in range(groups):
         members = slots[group * per_tile : (group + 1) * per_tile]
-        tabs = [jnp.zeros((SUBS, LANES), jnp.float32) for _ in range(2)]
         turn = jnp.zeros((SUBS, LANES), jnp.float32)
         for level in range(levels):
             for tap in range(taps):
-                hit = lane == tap * levels + level
                 for part in range(2):
-                    entry = by_member([coeffs_ref[part, row, level, tap] for row in members])
-                    tabs[part] = jnp.where(hit, entry, tabs[part])
+                    table_buf[table_at(group, tap, part, level), :] = by_member(
+                        [coeffs_ref[part, row, level, tap] for row in members]
+                    )
             turn = jnp.where(lane == level, by_member([angles_ref[row, level] for row in members]), turn)
-        coef_tabs.append(tabs)
-        cos_tabs.append(jnp.cos(turn))
-        sin_tabs.append(jnp.sin(turn))
-
-    def pick(table, index):
-        return jnp.take_along_axis(table, index, axis=1)
+        for which, tab in enumerate((jnp.cos(turn), jnp.sin(turn))):
+            turn_tabs.append([jnp.broadcast_to(tab[:, level : level + 1], (SUBS, LANES)) for level in range(levels)])
 
     def coef_at(group, y, tap, part):
         return tile_rows(((group * rows + y) * taps + tap) * 2 + part)
@@ -80,17 +79,28 @@
     def turn_at(group, y, which):
         return tile_rows((group * rows + y) * 2 + which)
 
-    @pl.loop(0, rows)
-    def _(y):
-        level_tile = level_buf[tile_rows(y), :]
+    def choose(masks, entries):
+        tile = entries[0]
+        for mask, entry in zip(masks, entries[1:]):
+            tile = jnp.where(mask, entry, tile)
+        return tile
+
+    @pl.loop(0, rows // PAIR)
+    def _(trip):
+        y = trip * PAIR
+        masks = []
+        for place in range(PAIR):
+            level_tile = level_buf[tile_rows(y + place), :]
+            masks.append([level_tile == level for level in range(1, levels)])
         for group in range(groups):
-            turn_buf[turn_at(group, y, 0), :] = pick(cos_tabs[group], level_tile)
-            turn_buf[turn_at(group, y, 1), :] = pick(sin_tabs[group], level_tile)
-        for tap in range(taps):
-            index = level_tile + tap * levels
-            for group in range(groups):
+            for which in range(2):
+                for place in range(PAIR):
+                    turn_buf[turn_at(group, y + place, which), :] = choose(masks[place], turn_tabs[group * 2 + which])
+            for tap in range(taps):
                 for part in range(2):
-                    coef_buf[coef_at(group, y, tap, part), :] = pick(coef_tabs[group][part], index)
+                    entries = [table_buf[table_at(group, tap, part, level), :] for level in range(levels)]
+                    for place in range(PAIR):
+                        coef_buf[coef_at(group, y + place, tap, part), :] = choose(masks[place], entries)
 
     def field_at(group, comp, y):
         return tile_rows((group * 4 + comp) * rows + y)
@@ -174,13 +184,14 @@
             acc[3] = acc[3] + cr * ri - ci * rr
 
     def inline_pass(step, group):
-        @pl.loop(0, half)
-        def _(y):
-            inline_row(step, group, y)
-
-        @pl.loop(rows - half, rows)
-        def _(y):
-            inline_row(step, group, y)
+        def inline_rows(first, last):
+            @pl.loop(first // ROWS, last // ROWS)
+            def _(trip):
+                for place in range(ROWS):
+                    inline_row(step, group, trip * ROWS + place)
+
+        inline_rows(0, half)
+        inline_rows(rows - half, rows)
 
         for side, there in enumerate((has_low, has_high)):
 
@@ -188,9 +199,7 @@
             def _():
                 halo_copy(step, group, side).start()
 
-        @pl.loop(half, rows - half)
-        def _(y):
-            inline_row(step, group, y)
+        inline_rows(half, rows - half)
 
     def cross_pass(step, group):
         for side, there in ((1, has_low), (0, has_high)):
@@ -275,6 +284,7 @@
         out_specs=(vmem, vmem),
         scratch_shapes=[
             pltpu.VMEM((rows * SUBS, LANES), jnp.int32),
+            tiles(groups * taps * 2 * level_count),
             tiles(groups * rows * taps * 2),
             tiles(groups * rows * 2),
             tiles(groups * 4 * rows),

time: 40.3 us -> 31.5 us (0.78)
  Pallas kernels: 35 us -> 26.1 us
    pallas_call x1, Pallas kernels: 35 us -> 26.1 us  [on_device(): pl.pallas_call(functools.partial(kernel, sizes), out_shape=(jax.ShapeDtyp...]
where the time goes in v1:
time: 31.5 us; the launch traced here: 31.2 us
  Pallas kernels  26.1 us (83%)
  local copies, waits for them, and re-layouts  4.44 us (14%)
  between operations  0.67 us (2%)
    pallas_call x1, Pallas kernels, on_device(): pl.pallas_call(functools.partial(kernel, sizes), out_shape=(jax.ShapeDtyp...  26.1 us
    unnamed x11, local copies, waits for them, and re-layouts  4.44 us

profile of v1, /device:TPU:9, one launch (start us, length us, event | category | flops | bytes accessed | tf_op | source)
XLA Modules:
  0.0 31.2 jit_solution(11749271165109426735)
XLA Ops:
  0.6 0.0 copy-start.3
  0.6 0.0 copy-start.2
  0.7 0.7 %copy.7.coeffs_ref = f32[2,4,5,17]{3,2,1,0:T(8,128)S(1)} copy(f32[2,4,5,17]{3,1,2,0:T(4,128)} %param.7) | data formatting | bytes 5440 | tf_op args[2]
  1.4 0.0 copy-done.3
  1.4 0.0 copy-done.2
  1.4 0.0 copy-start
  1.4 1.2 %copy-done = f32[2,2,4,32,512]{4,3,2,1,0:T(8,128)S(1)} copy-done((f32[2,2,4,32,512]{4,3,2,1,0:T(8,128)S(1)}, f32[2,2,4,32,512]{4,3,2,1,0:T(8,128)}, u32[]{:S(2)}) %copy-start) | copy-done | bytes 1048600
  2.6 0.0 copy-start.1
  2.6 0.8 %copy-done.1 = s32[32,512]{1,0:T(8,128)S(1)} copy-done((s32[32,512]{1,0:T(8,128)S(1)}, s32[32,512]{1,0:T(8,128)}, u32[]{:S(2)}) %copy-start.1) | copy-done | bytes 65560
  3.5 26.1 %shard_map.68 = (f32[2,2,4,32,512]{4,3,2,1,0:T(8,128)S(1)}, f32[2,32,512]{2,1,0:T(8,128)S(1)}) custom-call(f32[2,2,4,32,512]{4,3,2,1,0:T(8,128)S(1)} %copy-done, s32[32,512]{1,0:T(8,128)S(1)} %copy-done.1, f32[2,4,5,17]{3,2,1,0:T(8,128)S(1)} %copy.7.coeffs_ref, f32[4,5]{1,0:T(4,128)S(1)} %copy-done.2, s32[4]{0:T(128)S(1)} %copy-done.3), custom_call_target="tpu_custom_call" | custom-call | tf_op jit(solution)/shard_map/pallas_call | solution.py:277
  29.6 1.0 %copy.10 = f32[2,2,4,32,512]{4,3,2,1,0:T(8,128)} copy(f32[2,2,4,32,512]{4,3,2,1,0:T(8,128)S(1)} %get-tuple-element.4) | data formatting | bytes 2097152
  30.5 0.7 %copy.11 = f32[2,32,512]{2,1,0:T(8,128)} copy(f32[2,32,512]{2,1,0:T(8,128)S(1)} %get-tuple-element.5) | data formatting | bytes 262144
Async XLA Ops:
  0.6 0.8 %copy-start.3 = (s32[4]{0:T(128)S(1)}, s32[4]{0:T(128)}, u32[]{:S(2)}) copy-start(s32[4]{0:T(128)} %order_ref.1) | copy-start | bytes 52
  0.6 0.8 %copy-start.2 = (f32[4,5]{1,0:T(4,128)S(1)}, f32[4,5]{1,0:T(4,128)}, u32[]{:S(2)}) copy-start(f32[4,5]{1,0:T(4,128)} %angles_ref.1) | copy-start | bytes 244
  1.4 1.2 %copy-start = (f32[2,2,4,32,512]{4,3,2,1,0:T(8,128)S(1)}, f32[2,2,4,32,512]{4,3,2,1,0:T(8,128)}, u32[]{:S(2)}) copy-start(f32[2,2,4,32,512]{4,3,2,1,0:T(8,128)} %waves_ref.1) | copy-start | bytes 3145732
  2.6 0.8 %copy-start.1 = (s32[32,512]{1,0:T(8,128)S(1)}, s32[32,512]{1,0:T(8,128)}, u32[]{:S(2)}) copy-start(s32[32,512]{1,0:T(8,128)} %levels_ref.1) | copy-start | bytes 196612

commit v2 on v1

--- a/solution.py
+++ b/solution.py
@@ -10,7 +10,7 @@
 STEPS = 2
 LANES = 128
 SUBS = 8
-ROWS = 2
+ROWS = 4
 PAIR = 2
 MESH = pl.DeviceIdType.MESH
 
@@ -20,7 +20,8 @@
 
 
 def kernel(
-    sizes, waves_ref, levels_ref, coeffs_ref, angles_ref, order_ref, out_ref, image_ref,
+    sizes, waves_hbm, levels_hbm, coeffs_hbm, angles_ref, order_ref, out_ref, image_ref,
+    waves_ref, levels_ref, coeffs_ref, load_sem,
     level_buf, table_buf, coef_buf, turn_buf, field_buf, mid_buf, image_buf, send_sem, recv_sem,
 ):
     freqs, rows, blocks, per_tile, groups, levels, taps, strips = sizes
@@ -29,6 +30,15 @@
     me = lax.axis_index("strip")
     has_low, has_high = me > 0, me < strips - 1
 
+    loads = [
+        pltpu.make_async_copy(source, target, load_sem.at[i])
+        for i, (source, target) in enumerate(
+            ((coeffs_hbm, coeffs_ref), (levels_hbm, levels_ref), (waves_hbm, waves_ref))
+        )
+    ]
+    for load in loads:
+        load.start()
+
     def neighbour(step):
         return {"strip": me + step}
 
@@ -43,6 +53,7 @@
     sub = lax.broadcasted_iota(jnp.int32, (SUBS, LANES), 0)
     block_of = lax.rem(sub, blocks)
 
+    loads[1].wait()
     for top in range(0, rows, SUBS):
         for block in range(blocks):
             cells = levels_ref[top : top + SUBS, block * LANES : (block + 1) * LANES]
@@ -58,6 +69,7 @@
             tile = jnp.where(sub >= member * blocks, values[member], tile)
         return tile
 
+    loads[0].wait()
     slots = [order_ref[f] for f in range(freqs)]
     turn_tabs = []
     for group in range(groups):
@@ -108,6 +120,7 @@
     def mid_at(step, group, y, comp):
         return tile_rows(((step * groups + group) * span + y) * 4 + comp)
 
+    loads[2].wait()
     for group in range(groups):
         for comp in range(4):
             for member in range(per_tile):
@@ -183,55 +196,78 @@
             acc[2] = acc[2] + cr * rr + ci * ri
             acc[3] = acc[3] + cr * ri - ci * rr
 
-    def inline_pass(step, group):
-        def inline_rows(first, last):
-            @pl.loop(first // ROWS, last // ROWS)
-            def _(trip):
-                for place in range(ROWS):
-                    inline_row(step, group, trip * ROWS + place)
-
-        inline_rows(0, half)
-        inline_rows(rows - half, rows)
-
+    def trips(first, last, inline=None, cross=None):
+        @pl.loop(first // ROWS, last // ROWS)
+        def _(trip):
+            for place in range(ROWS):
+                if inline is not None:
+                    inline_row(*inline, trip * ROWS + place)
+                if cross is not None and place % PAIR == 0:
+                    cross_rows(*cross, trip * ROWS + place)
+
+    def send(step, group):
         for side, there in enumerate((has_low, has_high)):
 
             @pl.when(there)
             def _():
                 halo_copy(step, group, side).start()
 
-        inline_rows(half, rows - half)
-
-    def cross_pass(step, group):
+    def receive(step, group):
         for side, there in ((1, has_low), (0, has_high)):
 
             @pl.when(there)
             def _():
                 halo_copy(step, group, side).wait_recv()
 
-        @pl.loop(0, rows // PAIR)
-        def _(trip):
-            y = trip * PAIR
-            accs = [[None] * 4 for _ in range(PAIR)]
-            for line in range(taps + PAIR - 1):
-                moved = [mid_buf[mid_at(step, group, y + line, comp), :] for comp in range(4)]
-                for place in range(PAIR):
-                    if 0 <= line - place < taps:
-                        add_tap(accs[place], group, y + place, line - place, moved)
-            for place, acc in enumerate(accs):
-                for comp in range(4):
-                    field_buf[field_at(group, comp, y + place), :] = acc[comp]
-                term = acc[0] * acc[2] + acc[1] * acc[3]
-                at = tile_rows(step * rows + y + place)
-                if group == 0:
-                    image_buf[at, :] = term
-                else:
-                    image_buf[at, :] = image_buf[at, :] + term
-
-    for step in range(STEPS):
-        for group in range(groups):
-            inline_pass(step, group)
-        for group in range(groups):
-            cross_pass(step, group)
+    def cross_rows(step, group, y):
+        accs = [[None] * 4 for _ in range(PAIR)]
+        for line in range(taps + PAIR - 1):
+            moved = [mid_buf[mid_at(step, group, y + line, comp), :] for comp in range(4)]
+            for place in range(PAIR):
+                if 0 <= line - place < taps:
+                    add_tap(accs[place], group, y + place, line - place, moved)
+        for place, acc in enumerate(accs):
+            for comp in range(4):
+                field_buf[field_at(group, comp, y + place), :] = acc[comp]
+            term = acc[0] * acc[2] + acc[1] * acc[3]
+            at = tile_rows(step * rows + y + place)
+            if group == 0:
+                image_buf[at, :] = term
+            else:
+                image_buf[at, :] = image_buf[at, :] + term
+
+    passes = [(step, group) for step in range(STEPS) for group in range(groups)]
+    pending = []
+    for step, group in passes:
+        here = (step, group)
+        beside = None
+        if group == 0 and pending:
+            while len(pending) > 1 or pending[0][1] == 0:
+                before = pending.pop(0)
+                receive(*before)
+                trips(0, rows, cross=before)
+            before = pending.pop(0)
+            receive(*before)
+            trips(0, half, here, before)
+            trips(rows - half, rows, here, before)
+            send(*here)
+            trips(half, rows - half, here, before)
+        else:
+            trips(0, half, here)
+            trips(rows - half, rows, here)
+            send(*here)
+            if pending:
+                before = pending.pop(0)
+                receive(*before)
+                trips(half, rows - half, here, before)
+                trips(0, half, cross=before)
+                trips(rows - half, rows, cross=before)
+            else:
+                trips(half, rows - half, here)
+        pending.append(here)
+    for before in pending:
+        receive(*before)
+        trips(0, rows, cross=before)
 
     for group in range(groups):
         for comp in range(4):
@@ -273,16 +309,20 @@
     half = taps // 2
     sizes = (freqs, rows, blocks, per_tile, groups, level_count, taps, strips)
     tiles = lambda count: pltpu.VMEM((count * SUBS, LANES), jnp.float32)
-    vmem, smem = pl.BlockSpec(memory_space=pltpu.VMEM), pl.BlockSpec(memory_space=pltpu.SMEM)
+    vmem, smem, hbm = [pl.BlockSpec(memory_space=space) for space in (pltpu.VMEM, pltpu.SMEM, pltpu.HBM)]
     return pl.pallas_call(
         functools.partial(kernel, sizes),
         out_shape=(
             jax.ShapeDtypeStruct(waves.shape, jnp.float32),
             jax.ShapeDtypeStruct((STEPS, rows, cells), jnp.float32),
         ),
-        in_specs=[vmem, vmem, smem, smem, smem],
+        in_specs=[hbm, hbm, hbm, smem, smem],
         out_specs=(vmem, vmem),
         scratch_shapes=[
+            pltpu.VMEM(waves.shape, jnp.float32),
+            pltpu.VMEM(levels.shape, jnp.int32),
+            pltpu.SMEM(coeffs.shape, jnp.float32),
+            pltpu.SemaphoreType.DMA((3,)),
             pltpu.VMEM((rows * SUBS, LANES), jnp.int32),
             tiles(groups * taps * 2 * level_count),
             tiles(groups * rows * taps * 2),
@@ -294,7 +334,7 @@
             pltpu.SemaphoreType.DMA((STEPS, groups, 2)),
         ],
         compiler_params=pltpu.CompilerParams(
-            collective_id=0, has_side_effects=True, vmem_limit_bytes=48 * 1024 * 1024
+            collective_id=0, has_side_effects=True, vmem_limit_bytes=67043328 - 1250000
         ),
     )(waves, levels, coeffs, angles, order)
 

time: 31.5 us -> 30.4 us (0.965)
  Pallas kernels: 26.1 us -> 25.1 us
    pallas_call x1, Pallas kernels: 26.1 us -> 25.1 us  [on_device(): pl.pallas_call(functools.partial(kernel, sizes), out_shape=(jax.ShapeDtyp...]
    unnamed x11 -> x5, local copies, waits for them, and re-layouts: 4.44 us -> 4.33 us
where the time goes in v2:
time: 30.4 us; the launch traced here: 30.1 us
  Pallas kernels  25.1 us (83%)
  local copies, waits for them, and re-layouts  4.33 us (14%)
  between operations  0.65 us (2%)
    pallas_call x1, Pallas kernels, on_device(): pl.pallas_call(functools.partial(kernel, sizes), out_shape=(jax.ShapeDtyp...  25.1 us
    unnamed x5, local copies, waits for them, and re-layouts  4.33 us

profile of v2, /device:TPU:9, one launch (start us, length us, event | category | flops | bytes accessed | tf_op | source)
XLA Modules:
  0.0 30.1 jit_solution(6700932127013702524)
XLA Ops:
  0.6 1.4 %copy.7.coeffs_hbm = f32[2,4,5,17]{3,2,1,0:T(8,128)} copy(f32[2,4,5,17]{3,1,2,0:T(4,128)} %param.7) | data formatting | bytes 5440 | tf_op args[2]
  2.0 25.1 %shard_map.68 = (f32[2,2,4,32,512]{4,3,2,1,0:T(8,128)}, f32[2,32,512]{2,1,0:T(8,128)}) custom-call(f32[2,2,4,32,512]{4,3,2,1,0:T(8,128)} %waves_hbm.1, s32[32,512]{1,0:T(8,128)} %levels_hbm.1, f32[2,4,5,17]{3,2,1,0:T(8,128)} %copy.7.coeffs_hbm, f32[4,5]{1,0:T(4,128)} %angles_ref.1, s32[4]{0:T(128)} %order_ref.1), custom_call_target="tpu_custom_call" | custom-call | tf_op jit(solution)/shard_map/pallas_call | solution.py:313
  27.1 0.0 copy-start
  27.1 2.3 %copy.10 = f32[2,2,4,32,512]{4,3,2,1,0:T(8,128)} copy(f32[2,2,4,32,512]{4,3,2,1,0:T(8,128)} %get-tuple-element.4) | data formatting | bytes 2097152
  29.4 0.0 copy-done
  29.4 0.7 %copy.11 = f32[2,32,512]{2,1,0:T(8,128)} copy(f32[2,32,512]{2,1,0:T(8,128)S(1)} %copy-done) | data formatting | bytes 262144
Async XLA Ops:
  27.1 2.3 %copy-start = (f32[2,32,512]{2,1,0:T(8,128)S(1)}, f32[2,32,512]{2,1,0:T(8,128)}, u32[]{:S(2)}) copy-start(f32[2,32,512]{2,1,0:T(8,128)} %get-tuple-element.5) | copy-start | bytes 393220
